TPU v7x, 32 devices: a whole 2x2x4 slice. The times are simulated.
32 devices in a mesh: row: 4 (over y, x), col: 8 (over z, core).
Axes of the slice: x: 2, y: 2, z: 4, core: 2. Of those that a mesh axis runs over, the one named last changes fastest.
Arguments:
- anc_inverse: float32 [10240, 10240], P('row', 'col'), may hold values from -0.0625 to 0.0625
- lower_anc: float32 [10240, 3, 384], P('col', None, 'row'), may hold values from -1.5 to 1.5
- upper_anc: float32 [10240, 3, 384], P('row', None, 'col'), may hold values from -0.75 to 0.75
- lower_edge: float32 [2, 384, 384], replicated, may hold values from -0.3125 to 0.3125
- upper_edge: float32 [2, 384, 384], replicated, may hold values from -0.3125 to 0.3125
- diag_inverse: float32 [3, 384, 384], replicated, may hold values from -6 to 6
- tile_mask: int32 [3, 80, 3], replicated, may hold values 0 or 1
Outputs:
- x_blocks: float32 [10240, 3, 384], P(('row', 'col'))
- y_blocks: float32 [8, 4, 320, 3, 384], P('col', 'row')
- z_blocks: float32 [3, 384, 384], P(None, 'row', 'col')
- cross_blocks: float32 [2, 2, 384, 384], P(None, None, 'row', 'col')
All inputs are finite; a program needn't handle non-finite values.
Results may differ from a plain program's by a relative error of at most 0.0001.
Values sent between devices are 32-bit elements; how exact they have to be, the bound alone decides.
A program may use at most 128 MiB of HBM per device.

v0:
```python
import jax
import jax.numpy as jnp
from jax import lax
from jax.sharding import PartitionSpec as P

W = 384
BLK = 128
SUPER = 3
precise = lax.Precision.HIGHEST


def product(left, right):
    return jnp.dot(left, right, precision=precise, preferred_element_type=jnp.float32)


def inner_product(left, right):
    return lax.dot_general(
        left, right, (((0,), (0,)), ((), ())), precision=precise, preferred_element_type=jnp.float32
    )


def outer_product(left, right):
    return lax.dot_general(
        left, right, (((1,), (1,)), ((), ())), precision=precise, preferred_element_type=jnp.float32
    )


def tile_pattern(tile_mask, first_block, blocks):
    window = lax.dynamic_slice_in_dim(tile_mask, first_block, blocks, 1).astype(jnp.float32)
    window = jnp.transpose(window, (1, 0, 2))
    widened = jnp.broadcast_to(window[:, None, :, :, None], (blocks, BLK, SUPER, W // BLK, BLK))
    return widened.reshape(blocks * BLK, SUPER, W)


def row_term(anc_inverse, lower_cols):
    return product(anc_inverse, lower_cols)


def col_term(anc_inverse, upper_rows):
    return inner_product(anc_inverse, upper_rows)


def per_device(anc_inverse, lower_anc, upper_anc, lower_edge, upper_edge, diag_inverse, tile_mask):
    rows_here, cols_here = anc_inverse.shape
    slab_rows = rows_here // lax.axis_size("col")
    row_index = lax.axis_index("row")
    col_index = lax.axis_index("col")
    col_pattern = tile_pattern(tile_mask, col_index * (cols_here // BLK), cols_here // BLK)
    row_pattern = tile_pattern(tile_mask, row_index * (rows_here // BLK), rows_here // BLK)
    lower_list = []
    upper_list = []
    cols_list = []
    rows_list = []
    lower_full = lax.all_gather(lower_anc, "row", axis=2, tiled=True) * col_pattern
    upper_full = lax.all_gather(upper_anc, "col", axis=2, tiled=True) * row_pattern
    cols_all = lax.psum_scatter(
        row_term(anc_inverse, lower_full.reshape(cols_here, SUPER * W)),
        "col",
        scatter_dimension=0,
        tiled=True,
    )
    rows_all = lax.psum_scatter(
        col_term(anc_inverse, upper_full.reshape(rows_here, SUPER * W)),
        "row",
        scatter_dimension=0,
        tiled=True,
    )
    cols_all = cols_all.reshape(slab_rows, SUPER, W)
    rows_all = rows_all.reshape(slab_rows, SUPER, W)
    for node_index in range(SUPER):
        lower_list.append(lower_full[:, node_index, :])
        upper_list.append(upper_full[:, node_index, :])
        cols_list.append(cols_all[:, node_index, :])
        rows_list.append(rows_all[:, node_index, :])
    x_list = []
    y_list = []
    corner_list = []
    cross_cols = []
    cross_rows = []
    for node_index in range(SUPER):
        lower_cur = lower_list[node_index]
        upper_cur = upper_list[node_index]
        inv_cols = -cols_list[node_index]
        inv_rows = -rows_list[node_index]
        upper_mine = lax.dynamic_slice_in_dim(upper_cur, col_index * slab_rows, slab_rows, 0)
        if node_index > 0:
            lower_side = lower_edge[node_index - 1]
            upper_side = upper_edge[node_index - 1]
            lower_mine = lax.dynamic_slice_in_dim(lower_cur, row_index * slab_rows, slab_rows, 0)
            rows_lower = inner_product(prev_rows, lower_mine)
            upper_cols = inner_product(upper_mine, prev_cols)
        if node_index > 0:
            rows_lower, upper_cols = lax.psum((rows_lower, upper_cols), ("row", "col"))
        if node_index > 0:
            cross_col = -(rows_lower + product(prev_corner, lower_side))
            cross_row = -(upper_cols + product(upper_side, prev_corner))
            inv_cols = inv_cols - product(prev_cols, lower_side)
            inv_rows = inv_rows - outer_product(prev_rows, upper_side)
            cross_cols.append(cross_col)
            cross_rows.append(cross_row)
        inv_corner = diag_inverse[node_index] - lax.psum(
            inner_product(upper_mine, inv_cols), ("row", "col")
        )
        if node_index > 0:
            inv_corner = inv_corner - product(upper_side, cross_col)
        x_list.append(inv_cols)
        y_list.append(inv_rows)
        corner_list.append(inv_corner)
        prev_cols = inv_cols
        prev_rows = inv_rows
        prev_corner = inv_corner
    x_blocks = jnp.stack(x_list, axis=1)
    y_blocks = jnp.stack(y_list, axis=1)[None, None]
    tile_rows = W // lax.axis_size("row")
    tile_cols = W // lax.axis_size("col")
    corners = jnp.stack(corner_list)
    corners = lax.dynamic_slice_in_dim(corners, row_index * tile_rows, tile_rows, 1)
    z_blocks = lax.dynamic_slice_in_dim(corners, col_index * tile_cols, tile_cols, 2)
    crossed = jnp.stack([jnp.stack(cross_cols), jnp.stack(cross_rows)])
    crossed = lax.dynamic_slice_in_dim(crossed, row_index * tile_rows, tile_rows, 2)
    cross_blocks = lax.dynamic_slice_in_dim(crossed, col_index * tile_cols, tile_cols, 3)
    return (x_blocks, y_blocks, z_blocks, cross_blocks)


def solution(mesh):
    return jax.shard_map(
        per_device,
        mesh=mesh,
        in_specs=(
            P("row", "col"),
            P("col", None, "row"),
            P("row", None, "col"),
            P(),
            P(),
            P(),
            P(),
        ),
        out_specs=(
            P(("row", "col"), None, None),
            P("col", "row", None, None, None),
            P(None, "row", "col"),
            P(None, None, "row", "col"),
        ),
        check_vma=False,
    )
```

profile of v0, /device:TPU:0, one launch (start us, length us, event | category | flops | bytes accessed | tf_op | source)
XLA Modules:
  0.0 565.6 jit_solution(17613502817447202190)
XLA Ops:
  7.2 0.7 all-gather.3.cloned.1.call-update
  8.0 0.7 all-gather.5.cloned.1.call-update
  8.8 0.1 copy.69
  8.9 4.2 broadcast_in_dim.6
  13.1 10.5 %reshape.42 = f32[1280,3,384]{2,0,1:T(8,128)} reshape(f32[10,128,3,3,128]{4,3,1,0,2:T(4,128)} %broadcast_in_dim.6) | data formatting | bytes 11796480 | tf_op jit(solution)/shard_map/reshape | solution.py:32
  23.6 55.8 %all-gather.3.cloned.1.call-done = f32[1280,3,384]{0,2,1:T(8,128)} async-done(((f32[1280,3,96]{0,2,1:T(8,128)}), f32[1280,3,384]{0,2,1:T(8,128)}) %all-gather.3.cloned.1.call-update) | async-done | bytes 5898256 | tf_op jit(solution)/shard_map/all_gather | solution.py:54
  79.3 7.7 %copy.70 = f32[1280,3,384]{2,0,1:T(8,128)} copy(f32[1280,3,384]{0,2,1:T(8,128)} %all-gather.3.cloned.1.call-done) | data formatting | bytes 11796480 | tf_op jit(solution)/shard_map/all_gather | solution.py:54
  87.0 9.3 %mul.30 = f32[1280,3,384]{2,0,1:T(8,128)} multiply(f32[1280,3,384]{2,0,1:T(8,128)} %copy.70, f32[1280,3,384]{2,0,1:T(8,128)} %reshape.42) | non-fusion elementwise | flops 1474560 | bytes 17694720 | tf_op jit(solution)/shard_map/mul | solution.py:54
  96.3 7.8 %copy.71 = f32[1280,3,384]{0,2,1:T(8,128)} copy(f32[1280,3,384]{2,0,1:T(8,128)} %mul.30) | data formatting | bytes 11796480 | tf_op jit(solution)/shard_map/mul | solution.py:54
  104.0 52.7 %convolution_bitcast_fusion = f32[2560,1152]{0,1:T(8,128)} fusion(f32[1280,1152]{0,1:T(8,128)} %bitcast.163, f32[2560,1280]{1,0:T(8,128)} %param.7), kind=kOutput, calls=%fused_computation | convolution fusion | flops 45298483200 | bytes 30801920 | tf_op jit(solution)/shard_map/dot_general | solution.py:13
  156.8 13.6 %copy.92 = f32[2560,1152]{1,0:T(8,128)} copy(f32[2560,1152]{0,1:T(8,128)} %convolution_bitcast_fusion) | data formatting | bytes 23592960
  170.4 0.6 reduce-scatter.9.cloned.1.call-start
  171.1 6.0 %broadcast_in_dim.7 = f32[20,128,3,3,128]{1,0,4,3,2:T(8,128)} broadcast(f32[20,3,3]{0,2,1:T(4,128)S(1)} %convert_bitcast_fusion), dimensions={0,2,3} | broadcast | bytes 11797200 | tf_op jit(solution)/shard_map/broadcast_in_dim | solution.py:31
  177.1 13.7 %reshape.45 = f32[2560,3,384]{0,2,1:T(8,128)} reshape(f32[20,128,3,3,128]{1,0,4,3,2:T(8,128)} %broadcast_in_dim.7) | data formatting | bytes 23592960 | tf_op jit(solution)/shard_map/reshape | solution.py:32
  190.8 0.4 all-gather.5.cloned.1.call-done
  191.2 9.7 %mul.32 = f32[2560,3,384]{0,2,1:T(8,128)S(1)} multiply(f32[2560,3,384]{0,2,1:T(8,128)} %all-gather.5.cloned.1.call-done, f32[2560,3,384]{0,2,1:T(8,128)} %reshape.45) | non-fusion elementwise | flops 2949120 | bytes 35389440 | tf_op jit(solution)/shard_map/mul | solution.py:55
  200.9 4.3 copy-done
  205.3 50.1 %convolution_bitcast_fusion.1 = f32[1280,1152]{0,1:T(8,128)} fusion(f32[2560,1152]{0,1:T(8,128)S(1)} %bitcast.157, f32[2560,1280]{1,0:T(8,128)} %param.7), kind=kOutput, calls=%fused_computation.1 | convolution fusion | flops 45298483200 | bytes 30801920 | tf_op jit(solution)/shard_map/dot_general | solution.py:17
  255.4 7.7 %copy.94 = f32[1280,1152]{1,0:T(8,128)} copy(f32[1280,1152]{0,1:T(8,128)} %convolution_bitcast_fusion.1) | data formatting | bytes 11796480
  263.1 0.2 all-reduce.3.cloned.1.call-start
  263.3 4.3 fusion.75
  267.6 9.3 %fusion.74 = (f32[2560,1,384]{0,2,1:T(8,128)}, f32[2560,1,384]{0,2,1:T(8,128)}, f32[2560,1,384]{0,2,1:T(8,128)}) fusion(f32[2560,3,384]{0,2,1:T(8,128)} %copy-done), kind=kLoop, calls=%fused_computation.100 | loop fusion | bytes 23592960 | tf_op jit(solution)/shard_map/slice | solution.py:72
  276.9 36.6 %reduce-scatter.7.cloned.1.call-done = f32[320,1152]{1,0:T(8,128)} async-done(((f32[2560,1152]{1,0:T(8,128)}), f32[320,1152]{1,0:T(8,128)}) %reduce-scatter.7.cloned.1.call-update) | async-done | bytes 1474576
  313.5 2.1 copy.93
  315.6 0.9 fusion.77
  316.6 1.3 copy.96
  317.8 1.0 copy.97
  318.8 0.2 copy.98
  319.1 3.3 fusion.16
  322.4 1.1 convolution_subtract_fusion.3
  323.5 3.3 fusion.18
  326.7 3.3 fusion.12
  330.0 1.1 convolution_subtract_fusion.2
  331.1 0.8 copy-done.6
  331.9 3.2 fusion.14
  335.1 46.5 %reduce-scatter.9.cloned.1.call-done = f32[320,1152]{1,0:T(8,128)} async-done(((f32[1280,1152]{1,0:T(8,128)}), f32[320,1152]{1,0:T(8,128)}) %reduce-scatter.9.cloned.1.call-update) | async-done | bytes 1474576
  381.6 2.3 copy.95
  384.0 1.3 fusion.76
  385.2 1.4 copy.99
  386.6 2.1 copy.100
  388.7 3.3 fusion.20
  392.0 1.1 convolution_subtract_fusion.1
  393.1 3.2 fusion.49
  396.3 3.2 fusion.47
  399.5 0.8 neg.53
  400.4 0.8 neg.59
  401.2 1.3 copy.101
  402.5 2.2 pad_maximum_fusion
  404.7 1.1 fusion.11
  405.8 1.2 maximum_bitcast_fusion
  407.0 137.7 %all-reduce.3.cloned.1.call-done = (f32[384,384]{1,0:T(8,128)}, f32[384,384]{1,0:T(8,128)}, f32[384,384]{1,0:T(8,128)}, f32[384,384]{1,0:T(8,128)}, f32[384,384]...) async-done(((f32[384,384]{1,0:T(8,128)}, f32[384,384]{1,0:T(8,128)}, f32[384,384]{1,0:T(8,128)}, f32[384,384]{1,0:T(8,128)}, f32[384,384]{1,0:T(8,128)}, ...) | async-done | bytes 4128784 | tf_op jit(solution)/shard_map/psum | solution.py:101
  544.7 1.4 fusion.73
  546.2 0.1 copy-done.15
  546.3 2.5 fusion.7
  548.9 1.3 fusion
  550.2 1.3 fusion.10
  551.5 1.6 fusion.4
  553.1 1.3 fusion.1
  554.3 0.2 maximum_bitcast_fusion.1
  554.5 0.1 fusion.58
  554.7 0.7 copy.85
  555.4 2.5 fusion.9
  557.9 0.1 fusion.60
  558.1 0.7 copy.84
  (39 shorter events, 0.4 us)
Async XLA Ops:
  7.2 1.5 copy-start.16
  7.2 72.2 %all-gather.3.cloned.1.call-start = ((), (), s32[]{:S(2)}) async-start(), calls=%async_computation.2 | async-start | bytes 7372800 | tf_op jit(solution)/shard_map/all_gather | solution.py:54
  7.9 183.3 %all-gather.5.cloned.1.call-start = ((), (), s32[]{:S(2)}) async-start(), calls=%async_computation.3 | async-start | bytes 13271040 | tf_op jit(solution)/shard_map/all_gather | solution.py:55
  8.7 304.8 %reduce-scatter.7.cloned.1.call-start = ((), (), s32[]{:S(2)}) async-start(), calls=%async_computation.4 | async-start | bytes 13271040
  170.4 211.2 %reduce-scatter.9.cloned.1.call-start = ((), (), s32[]{:S(2)}) async-start(), calls=%async_computation.5 | async-start | bytes 7372800
  200.9 4.3 copy-start
  263.1 281.6 %all-reduce.3.cloned.1.call-start = ((), (), s32[]{:S(2)}) async-start(), calls=%async_computation.6 | async-start | bytes 8257536 | tf_op jit(solution)/shard_map/psum | solution.py:101
  317.8 4.5 copy-start.4
  319.1 3.3 copy-start.9
  331.1 0.8 copy-start.6
  385.2 6.8 %copy-start.1 = (f32[2,384,384]{2,1,0:T(8,128)S(1)}, f32[2,384,384]{2,1,0:T(8,128)}, u32[]{:S(2)}) copy-start(f32[2,384,384]{2,1,0:T(8,128)} %param.11) | copy-start | bytes 3538948
  388.7 3.3 copy-start.10
  400.4 2.1 copy-start.7
  404.7 1.1 copy-start.8
  544.7 1.5 copy-start.2
  544.7 1.6 copy-start.15
  544.7 4.2 copy-start.14
  546.1 2.7 copy-start.3
  546.1 2.7 copy-start.5
  548.8 1.3 copy-start.13
  550.1 1.3 copy-start.12
  551.5 1.6 copy-start.11
Sparse Core Ops, SparseCore 0:
  9.8 69.4 all-gather.2
  81.0 110.1 all-gather.4
  193.5 119.9 reduce-scatter.6
  316.4 65.2 reduce-scatter.8
  399.6 144.9 all-reduce.2
where the time goes:
time: 574 us; the launch traced here: 566 us
  waiting for transfers between devices  278 us (48%)
  matrix products  140 us (24%)
  local copies, waits for them, and re-layouts  105 us (18%)
  other arithmetic  26.1 us (5%)
  between operations  14.4 us (3%)
    psum x1, waiting for transfers between devices, per_device(): lax.psum(inner_product(upper_mine, inv_cols), ('row', 'col'))  138 us
    unnamed x7, waiting for transfers between devices  84.6 us
    dot_general x8, matrix products, inner_product(): lax.dot_general(left, right, (((0,), (0,)), ((), ())), precision=precise,...  72.9 us
    dot_general x9, matrix products, product(): jnp.dot(left, right, precision=precise, preferred_element_type=jnp.float32)  65.3 us
    all_gather x1, waiting for transfers between devices, per_device(): lax.all_gather(lower_anc, 'row', axis=2, tiled=True) * col_pattern  55.8 us
    unnamed x46, local copies, waits for them, and re-layouts  39.8 us
    reshape x2, local copies, waits for them, and re-layouts, tile_pattern(): return widened.reshape(blocks * BLK, SUPER, W)  24.2 us
  transfers between devices with their start and end apart: 5, of which 5 were waited for; matrix products, arithmetic and copies ran while one was open for 42% of the time, Pallas kernels for 0%

commit v1 on v0

--- a/solution.py
+++ b/solution.py
@@ -1,3 +1,4 @@
+import functools
 import jax
 import jax.numpy as jnp
 from jax import lax
@@ -7,6 +8,13 @@
 BLK = 128
 SUPER = 3
 precise = lax.Precision.HIGHEST
+
+
+def scan_shifts_all(frame, mesh_name, shard_axis):
+    return lax.psum(lax.psum(frame, axis_name=mesh_name), axis_name=shard_axis)
+
+
+prepare_things_over_axis = functools.partial(scan_shifts_all, mesh_name="row", shard_axis="col")
 
 
 def product(left, right):
@@ -98,8 +106,8 @@
             inv_rows = inv_rows - outer_product(prev_rows, upper_side)
             cross_cols.append(cross_col)
             cross_rows.append(cross_row)
-        inv_corner = diag_inverse[node_index] - lax.psum(
-            inner_product(upper_mine, inv_cols), ("row", "col")
+        inv_corner = diag_inverse[node_index] - prepare_things_over_axis(
+            inner_product(upper_mine, inv_cols)
         )
         if node_index > 0:
             inv_corner = inv_corner - product(upper_side, cross_col)

time: 574 us -> 686 us (1.20)
  waiting for transfers between devices: 278 us -> 388 us
    psum x1 -> x3, waiting for transfers between devices: 138 us -> 245 us  [the longest x1 140 us: per_device(): rows_lower, upper_cols = lax.psum((rows_lower, upper_cols), ('row', 'col'))]
    unnamed x7 -> x9, waiting for transfers between devices: 84.6 us -> 86.7 us
    unnamed x46 -> x48, local copies, waits for them, and re-layouts: 39.8 us -> 40.2 us
  transfers between devices with their start and end apart: 5 -> 7, of which waited for: 5 -> 7; matrix products, arithmetic and copies ran while one was open for 42% -> 38% of each run, Pallas kernels for 0% -> 0%
where the time goes in v1:
time: 686 us; the launch traced here: 678 us
  waiting for transfers between devices  388 us (57%)
  matrix products  142 us (21%)
  local copies, waits for them, and re-layouts  106 us (15%)
  other arithmetic  26.8 us (4%)
  between operations  14.7 us (2%)
    psum x1, waiting for transfers between devices, per_device(): rows_lower, upper_cols = lax.psum((rows_lower, upper_cols), ('row', 'col'))  140 us
    psum x2, waiting for transfers between devices, scan_shifts_all(): return lax.psum(lax.psum(frame, axis_name=mesh_name), axis_name=shard_axis)  104 us
    unnamed x9, waiting for transfers between devices  86.7 us
    dot_general x8, matrix products, inner_product(): lax.dot_general(left, right, (((0,), (0,)), ((), ())), precision=precise,...  72.9 us
    dot_general x9, matrix products, product(): jnp.dot(left, right, precision=precise, preferred_element_type=jnp.float32)  66.6 us
    all_gather x1, waiting for transfers between devices, per_device(): lax.all_gather(lower_anc, 'row', axis=2, tiled=True) * col_pattern  55.8 us
    unnamed x48, local copies, waits for them, and re-layouts  40.2 us
    reshape x2, local copies, waits for them, and re-layouts, tile_pattern(): return widened.reshape(blocks * BLK, SUPER, W)  24.2 us
  transfers between devices with their start and end apart: 7, of which 7 were waited for; matrix products, arithmetic and copies ran while one was open for 38% of the time, Pallas kernels for 0%

profile of v1, /device:TPU:0, one launch (start us, length us, event | category | flops | bytes accessed | tf_op | source)
XLA Modules:
  0.0 678.1 jit_solution(10047596744527097252)
XLA Ops:
  7.2 0.7 all-gather.3.cloned.1.call-update
  8.0 0.7 all-gather.5.cloned.1.call-update
  8.9 4.1 broadcast_in_dim.6
  13.1 10.5 %reshape.42 = f32[1280,3,384]{2,0,1:T(8,128)} reshape(f32[10,128,3,3,128]{4,3,1,0,2:T(4,128)} %broadcast_in_dim.6) | data formatting | bytes 11796480 | tf_op jit(solution)/shard_map/reshape | solution.py:40
  23.5 55.8 %all-gather.3.cloned.1.call-done = f32[1280,3,384]{0,2,1:T(8,128)} async-done(((f32[1280,3,96]{0,2,1:T(8,128)}), f32[1280,3,384]{0,2,1:T(8,128)}) %all-gather.3.cloned.1.call-update) | async-done | bytes 5898256 | tf_op jit(solution)/shard_map/all_gather | solution.py:62
  79.3 7.7 %copy.70 = f32[1280,3,384]{2,0,1:T(8,128)} copy(f32[1280,3,384]{0,2,1:T(8,128)} %all-gather.3.cloned.1.call-done) | data formatting | bytes 11796480 | tf_op jit(solution)/shard_map/all_gather | solution.py:62
  87.0 9.3 %mul.30 = f32[1280,3,384]{2,0,1:T(8,128)} multiply(f32[1280,3,384]{2,0,1:T(8,128)} %copy.70, f32[1280,3,384]{2,0,1:T(8,128)} %reshape.42) | non-fusion elementwise | flops 1474560 | bytes 17694720 | tf_op jit(solution)/shard_map/mul | solution.py:62
  96.3 7.8 %copy.71 = f32[1280,3,384]{0,2,1:T(8,128)} copy(f32[1280,3,384]{2,0,1:T(8,128)} %mul.30) | data formatting | bytes 11796480 | tf_op jit(solution)/shard_map/mul | solution.py:62
  104.0 52.7 %convolution_bitcast_fusion = f32[2560,1152]{0,1:T(8,128)} fusion(f32[1280,1152]{0,1:T(8,128)} %bitcast.163, f32[2560,1280]{1,0:T(8,128)} %param.7), kind=kOutput, calls=%fused_computation | convolution fusion | flops 45298483200 | bytes 30801920 | tf_op jit(solution)/shard_map/dot_general | solution.py:21
  156.7 13.6 %copy.92 = f32[2560,1152]{1,0:T(8,128)} copy(f32[2560,1152]{0,1:T(8,128)} %convolution_bitcast_fusion) | data formatting | bytes 23592960
  170.3 0.6 reduce-scatter.9.cloned.1.call-start
  171.0 6.0 broadcast_in_dim.7
  177.0 13.7 %reshape.45 = f32[2560,3,384]{0,2,1:T(8,128)} reshape(f32[20,128,3,3,128]{1,0,4,3,2:T(8,128)} %broadcast_in_dim.7) | data formatting | bytes 23592960 | tf_op jit(solution)/shard_map/reshape | solution.py:40
  190.7 0.5 all-gather.5.cloned.1.call-done
  191.2 9.7 %mul.32 = f32[2560,3,384]{0,2,1:T(8,128)S(1)} multiply(f32[2560,3,384]{0,2,1:T(8,128)} %all-gather.5.cloned.1.call-done, f32[2560,3,384]{0,2,1:T(8,128)} %reshape.45) | non-fusion elementwise | flops 2949120 | bytes 35389440 | tf_op jit(solution)/shard_map/mul | solution.py:63
  200.9 4.3 copy-done
  205.3 50.1 %convolution_bitcast_fusion.1 = f32[1280,1152]{0,1:T(8,128)} fusion(f32[2560,1152]{0,1:T(8,128)S(1)} %bitcast.157, f32[2560,1280]{1,0:T(8,128)} %param.7), kind=kOutput, calls=%fused_computation.1 | convolution fusion | flops 45298483200 | bytes 30801920 | tf_op jit(solution)/shard_map/dot_general | solution.py:25
  255.4 7.7 %copy.94 = f32[1280,1152]{1,0:T(8,128)} copy(f32[1280,1152]{0,1:T(8,128)} %convolution_bitcast_fusion.1) | data formatting | bytes 11796480
  263.1 0.2 all-reduce.11.cloned.1.call-start
  263.3 9.2 %fusion.74 = (f32[2560,1,384]{0,2,1:T(8,128)}, f32[2560,1,384]{0,2,1:T(8,128)}, f32[2560,1,384]{0,2,1:T(8,128)}) fusion(f32[2560,3,384]{0,2,1:T(8,128)} %copy-done), kind=kLoop, calls=%fused_computation.100 | loop fusion | bytes 23592960 | tf_op jit(solution)/shard_map/slice | solution.py:80
  272.6 40.9 %reduce-scatter.7.cloned.1.call-done = f32[320,1152]{1,0:T(8,128)} async-done(((f32[2560,1152]{1,0:T(8,128)}), f32[320,1152]{1,0:T(8,128)}) %reduce-scatter.7.cloned.1.call-update) | async-done | bytes 1474576
  313.5 2.1 copy.93
  315.6 0.9 fusion.77
  316.6 1.3 copy.96
  317.8 1.0 copy.97
  318.8 1.0 copy.98
  319.8 3.3 fusion.20
  323.1 1.1 convolution_subtract_fusion.3
  324.2 3.3 fusion.18
  327.4 1.1 convolution_subtract_fusion.2
  328.5 0.8 copy-done.7
  329.3 3.3 fusion.14
  332.7 4.6 fusion.75
  337.3 44.4 %reduce-scatter.9.cloned.1.call-done = f32[320,1152]{1,0:T(8,128)} async-done(((f32[1280,1152]{1,0:T(8,128)}), f32[320,1152]{1,0:T(8,128)}) %reduce-scatter.9.cloned.1.call-update) | async-done | bytes 1474576
  381.6 2.1 copy.95
  383.8 3.3 fusion.12
  387.0 1.2 fusion.76
  388.3 60.7 %all-reduce.11.cloned.1.call-done = (f32[384,384]{1,0:T(8,128)}, f32[384,384]{1,0:T(8,128)}, f32[384,384]{1,0:T(8,128)}) async-done(((f32[384,384]{1,0:T(8,128)}, f32[384,384]{1,0:T(8,128)}, f32[384,384]{1,0:T(8,128)}), (f32[384,384]{1,0:T(8,128)}, f32[384,384]{1,0:T(8,128)}, f32[384,384]{1,0:T(8,128)})) %all-reduce.11.cloned.1.call-update) | async-done | bytes 1769488 | tf_op jit(solution)/shard_map/psum | solution.py:14
  449.1 0.3 all-reduce.7.cloned.1.call-start
  449.3 3.3 fusion.16
  452.6 1.4 copy.99
  453.9 2.1 copy.100
  456.0 3.3 fusion.49
  459.3 1.1 convolution_subtract_fusion.1
  460.4 3.2 fusion.47
  463.7 0.8 neg.53
  464.5 0.8 neg.59
  465.3 1.3 copy.101
  466.6 2.2 pad_maximum_fusion
  468.8 1.1 fusion.11
  469.9 1.2 maximum_bitcast_fusion
  471.1 43.7 %all-reduce.9.cloned.1.call-done = (f32[384,384]{1,0:T(8,128)}, f32[384,384]{1,0:T(8,128)}, f32[384,384]{1,0:T(8,128)}) async-done(((f32[384,384]{1,0:T(8,128)}, f32[384,384]{1,0:T(8,128)}, f32[384,384]{1,0:T(8,128)}), (f32[384,384]{1,0:T(8,128)}, f32[384,384]{1,0:T(8,128)}, f32[384,384]{1,0:T(8,128)})) %all-reduce.9.cloned.1.call-update) | async-done | bytes 1769488 | tf_op jit(solution)/shard_map/psum | solution.py:14
  514.9 2.2 fusion.73
  517.0 140.0 %all-reduce.7.cloned.1.call-done = (f32[384,384]{1,0:T(8,128)}, f32[384,384]{1,0:T(8,128)}, f32[384,384]{1,0:T(8,128)}, f32[384,384]{1,0:T(8,128)}) async-done(((f32[384,384]{1,0:T(8,128)}, f32[384,384]{1,0:T(8,128)}, f32[384,384]{1,0:T(8,128)}, f32[384,384]{1,0:T(8,128)}), (f32[384,384]{1,0:T(8,128)}, f32[384,384]{1,0:T(8,128)}, f32[384,384]{1,0:T(8,128)}, ...) | async-done | bytes 2359312 | tf_op jit(solution)/shard_map/psum | solution.py:101
  657.1 2.7 fusion.7
  659.8 2.4 fusion
  662.2 1.3 fusion.10
  663.6 1.6 fusion.4
  665.2 1.3 fusion.1
  666.5 0.2 maximum_bitcast_fusion.1
  666.7 0.1 fusion.58
  666.8 0.7 copy.85
  667.6 2.5 fusion.9
  670.2 0.7 copy.84
  (47 shorter events, 0.7 us)
Async XLA Ops:
  7.2 1.5 copy-start.17
  7.2 72.2 %all-gather.3.cloned.1.call-start = ((), (), s32[]{:S(2)}) async-start(), calls=%async_computation.2 | async-start | bytes 7372800 | tf_op jit(solution)/shard_map/all_gather | solution.py:62
  7.9 183.3 %all-gather.5.cloned.1.call-start = ((), (), s32[]{:S(2)}) async-start(), calls=%async_computation.3 | async-start | bytes 13271040 | tf_op jit(solution)/shard_map/all_gather | solution.py:63
  8.7 304.8 %reduce-scatter.7.cloned.1.call-start = ((), (), s32[]{:S(2)}) async-start(), calls=%async_computation.4 | async-start | bytes 13271040
  170.3 211.3 %reduce-scatter.9.cloned.1.call-start = ((), (), s32[]{:S(2)}) async-start(), calls=%async_computation.5 | async-start | bytes 7372800
  200.9 4.3 copy-start
  263.1 185.9 %all-reduce.11.cloned.1.call-start = ((), (), s32[]{:S(2)}) async-start(), calls=%async_computation.8 | async-start | bytes 3538944 | tf_op jit(solution)/shard_map/psum | solution.py:14
  317.8 5.3 copy-start.4
  318.8 4.3 copy-start.11
  323.1 4.3 copy-start.12
  328.5 0.8 copy-start.7
  332.6 182.2 %all-reduce.9.cloned.1.call-start = ((), (), s32[]{:S(2)}) async-start(), calls=%async_computation.7 | async-start | bytes 3538944 | tf_op jit(solution)/shard_map/psum | solution.py:14
  449.1 208.0 %all-reduce.7.cloned.1.call-start = ((), (), s32[]{:S(2)}) async-start(), calls=%async_computation.6 | async-start | bytes 4718592 | tf_op jit(solution)/shard_map/psum | solution.py:101
  452.6 6.8 copy-start.1
  456.0 3.3 copy-start.13
  464.5 2.1 copy-start.8
  468.8 1.1 copy-start.10
  514.9 142.2 %copy-start.2 = (f32[384,384]{1,0:T(8,128)S(1)}, f32[384,384]{1,0:T(8,128)}, u32[]{:S(2)}) copy-start(f32[384,384]{1,0:T(8,128)} %get-tuple-element.28) | copy-start | bytes 1769476
  517.0 142.8 %copy-start.5 = (f32[2,384,384]{2,1,0:T(8,128)S(1)}, f32[2,384,384]{2,1,0:T(8,128)}, u32[]{:S(2)}) copy-start(f32[2,384,384]{2,1,0:T(8,128)} %param.10) | copy-start | bytes 3538948
  657.1 2.7 copy-start.3
  659.8 2.4 copy-start.14
  662.2 1.4 copy-start.16
  663.6 1.6 copy-start.6
  663.6 1.6 copy-start.15
  666.8 3.3 copy-start.9
Sparse Core Ops, SparseCore 0:
  9.8 69.4 all-gather.2
  81.0 110.1 all-gather.4
  193.5 119.9 reduce-scatter.6
  316.4 65.2 reduce-scatter.8
  384.9 64.0 all-reduce.10
  451.5 63.3 all-reduce.8
  520.9 136.1 all-reduce.6
